TPU v7x, 128 devices: a whole 4x4x4 slice. The times are simulated.
128 devices in a mesh: expert: 16 (over x, y), head: 8 (over z, core).
Axes of the slice: x: 4, y: 4, z: 4, core: 2. Of those that a mesh axis runs over, the one named last changes fastest.
Arguments:
- table_cells: bfloat16 [8192, 2, 2048], P(('expert', 'head')), may hold values from -8 to 8
- w_query: bfloat16 [2048, 2048], P(None, 'head')
- w_key: bfloat16 [2048, 2048], P(None, 'head')
- w_value: bfloat16 [2048, 2048], P(None, 'head'), may hold values from -0.125 to 0.125
- w_out: bfloat16 [2048, 2048], P('head'), may hold values from -0.125 to 0.125
- norm_gain: bfloat16 [2048], replicated, may hold values from 0.099609375 to 1.8984375
- w_gate: bfloat16 [128, 704, 2048], P(('expert', 'head')), may hold values from -0.125 to 0.125
- w_up: bfloat16 [128, 704, 2048], P(('expert', 'head')), may hold values from -0.125 to 0.125
- w_down: bfloat16 [128, 704, 2048], P(('expert', 'head')), may hold values from -0.15625 to 0.15625
- lengths: int32 [2], replicated, may hold values from 2048 to 8192, as said below
- expert_of_cell: int32 [8192, 2], P(('expert', 'head')), may hold values from 0 to 63, as said below
- slot_of_cell: int32 [8192, 2], P(('expert', 'head')), may hold values from 0 to 3, as said below
Outputs:
- updated_cells: bfloat16 [8192, 2, 2048], P(('expert', 'head'))
Inputs may be any that keep to these rules, and one draw needn't show every extreme that they name: `lengths`: one table in every draw has all 8192 cells. `expert_of_cell`: within the 128 cells of one device (aligned blocks in row-major order), no expert has more than 4 cells, and in every draw one expert has exactly 4 cells in every device's block. `slot_of_cell`: cells of one device with the same expert have distinct slots.
All inputs are finite; a program needn't handle non-finite values.
Results may differ from a plain program's by a relative error of at most 0.014.
Values may be sent and summed in bfloat16 or wider, within the bound.
A program may use at most 128 MiB of HBM per device.

v0:
```python
import math
import jax
import jax.numpy as jnp
from jax import lax
from jax.sharding import PartitionSpec as P

DH = 128


def expert_half(slot_rows, gate_half, up_half, down_half):
    contract_rows = (((1,), (1,)), ((), ()))
    gate_t = lax.dot_general(
        gate_half, slot_rows, contract_rows, preferred_element_type=jnp.float32
    )
    up_t = lax.dot_general(up_half, slot_rows, contract_rows, preferred_element_type=jnp.float32)
    hidden = (jax.nn.silu(gate_t) * up_t).astype(jnp.bfloat16)
    product = lax.dot_general(
        hidden, down_half, (((0,), (0,)), ((), ())), preferred_element_type=jnp.float32
    )
    return product.astype(jnp.bfloat16)


def shards(
    table_cells,
    w_query,
    w_key,
    w_value,
    w_out,
    norm_gain,
    w_gate,
    w_up,
    w_down,
    lengths,
    expert_of_cell,
    slot_of_cell,
):
    cell_count, tables, model_width = table_cells.shape
    head_width = w_query.shape[1]
    head_count = head_width // DH
    score_scale = 1.0 / math.sqrt(DH)
    joined = jnp.concatenate([w_query, w_key, w_value], axis=1)
    shard_rows = lax.all_gather(table_cells, "head", axis=0, tiled=True)
    rows_here = shard_rows.shape[0]
    mixed_rows = jnp.dot(
        shard_rows.reshape(rows_here * tables, model_width),
        joined,
        preferred_element_type=jnp.float32,
    )
    projected = mixed_rows.astype(jnp.bfloat16).reshape(rows_here, tables, 3 * head_width)
    row_cells = projected.shape[0]
    queries = projected[:, :, :head_width].reshape(row_cells, tables, head_count, DH)
    key_rows = projected[:, :, head_width : 2 * head_width]
    value_rows = projected[:, :, 2 * head_width :]
    offset = lax.axis_index("expert") * row_cells
    own_positions = offset + jnp.arange(row_cells, dtype=jnp.int32)
    start_state = (
        jnp.full((tables, head_count, row_cells), -1e30, jnp.float32),
        jnp.zeros((tables, head_count, row_cells), jnp.float32),
        jnp.zeros((tables, head_count, row_cells, DH), jnp.float32),
    )
    key_piece = lax.all_gather(key_rows, "expert", axis=0, tiled=True)
    value_piece = lax.all_gather(value_rows, "expert", axis=0, tiled=True)
    piece_len = key_piece.shape[0]
    block_len = math.gcd(piece_len, 512)
    block_count = piece_len // block_len
    key_blocks = key_piece.reshape(block_count, block_len, tables, head_count, DH)
    value_blocks = value_piece.reshape(block_count, block_len, tables, head_count, DH)
    block_starts = jnp.arange(block_count, dtype=jnp.int32) * block_len

    def step(carried, block_item):
        running_max, running_sum, accum = carried
        key_block, value_block, block_first = block_item
        scores = (
            jnp.einsum("qshd,kshd->shqk", queries, key_block, preferred_element_type=jnp.float32)
            * score_scale
        )
        key_valid = (block_first + jnp.arange(block_len, dtype=jnp.int32))[None, :] < lengths[
            :, None
        ]
        scores = jnp.where(key_valid[:, None, None, :], scores, -jnp.inf)
        new_max = jnp.maximum(running_max, jnp.max(scores, axis=-1))
        factor = jnp.exp(running_max - new_max)
        exp_scores = jnp.exp(scores - new_max[..., None])
        running_sum = running_sum * factor + jnp.sum(exp_scores, axis=-1)
        accum = accum * factor[..., None] + jnp.einsum(
            "shqk,kshd->shqd",
            exp_scores.astype(jnp.bfloat16),
            value_block,
            preferred_element_type=jnp.float32,
        )
        return ((new_max, running_sum, accum), None)

    finished, _ = lax.scan(step, start_state, (key_blocks, value_blocks, block_starts))
    running_max, running_sum, accum = finished
    normalized = accum / running_sum[..., None]
    live = own_positions[None, :] < lengths[:, None]
    normalized = jnp.where(live[:, None, :, None], normalized, 0.0)
    attended = (
        jnp.transpose(normalized, (2, 0, 1, 3))
        .reshape(row_cells, tables, head_width)
        .astype(jnp.bfloat16)
    )
    count_rows = cell_count * lax.axis_size("head")
    product = jnp.dot(
        attended.reshape(count_rows * tables, head_width), w_out, preferred_element_type=jnp.float32
    )
    summed = lax.psum_scatter(
        product.reshape(count_rows, tables, model_width).astype(jnp.bfloat16),
        "head",
        scatter_dimension=0,
        tiled=True,
    ).astype(jnp.float32)
    residual = table_cells.astype(jnp.float32) + summed
    mean_square = jnp.mean(residual * residual, axis=-1, keepdims=True)
    normed = (residual * lax.rsqrt(mean_square + 1e-06) * norm_gain.astype(jnp.float32)).astype(
        jnp.bfloat16
    )
    rows_dev = cell_count * tables
    normed_rows = normed.reshape(rows_dev, model_width)
    expert_count = lax.axis_size("expert") * lax.axis_size("head") // 2
    slot_cap = 2 * max(1, rows_dev // expert_count)
    target = expert_of_cell.reshape(rows_dev) * slot_cap + slot_of_cell.reshape(rows_dev)
    slot_table = (
        jnp.arange(expert_count * slot_cap, dtype=jnp.int32)[:, None] == target[None, :]
    ).astype(jnp.bfloat16)
    send_rows = jnp.dot(slot_table, normed_rows, preferred_element_type=jnp.float32).astype(
        jnp.bfloat16
    )
    gate_half = w_gate[0]
    up_half = w_up[0]
    down_half = w_down[0]
    doubled = jnp.repeat(send_rows.reshape(expert_count, slot_cap, model_width), 2, axis=0)
    received = lax.all_to_all(doubled, ("expert", "head"), split_axis=0, concat_axis=0, tiled=True)
    sources = received.shape[0]
    item_count = received.shape[1]
    flat_rows = received.reshape(sources * item_count, model_width)
    gathered = lax.all_to_all(
        expert_half(flat_rows, gate_half, up_half, down_half).reshape(
            sources, item_count, model_width
        ),
        ("expert", "head"),
        split_axis=0,
        concat_axis=0,
        tiled=True,
    )
    halves = gathered.reshape(expert_count, 2, slot_cap, model_width).astype(jnp.float32)
    combined = (
        (halves[:, 0] + halves[:, 1])
        .astype(jnp.bfloat16)
        .reshape(expert_count * slot_cap, model_width)
    )
    expert_out = lax.dot_general(
        slot_table, combined, (((0,), (0,)), ((), ())), preferred_element_type=jnp.float32
    )
    updated = (residual.reshape(rows_dev, model_width) + expert_out).astype(jnp.bfloat16)
    return updated.reshape(cell_count, tables, model_width)


def solution(mesh):
    placed = (
        P(("expert", "head"), None, None),
        P(None, "head"),
        P(None, "head"),
        P(None, "head"),
        P("head", None),
        P(),
        P(("expert", "head"), None, None),
        P(("expert", "head"), None, None),
        P(("expert", "head"), None, None),
        P(),
        P(("expert", "head"), None),
        P(("expert", "head"), None),
    )
    return jax.shard_map(
        shards,
        mesh=mesh,
        in_specs=placed,
        out_specs=P(("expert", "head"), None, None),
        check_vma=False,
    )
```

profile of v0, /device:TPU:1, one launch (start us, length us, event | category | flops | bytes accessed | tf_op | source)
XLA Modules:
  0.0 631.7 jit_solution(11269988385761301558)
XLA Ops:
  7.3 37.8 %all-gather.4.cloned.1.call-done = bf16[512,2,2048]{2,1,0:T(2,128)(2,1)} async-done(((bf16[64,2,2048]{2,1,0:T(2,128)(2,1)}), bf16[512,2,2048]{2,1,0:T(2,128)(2,1)}) %all-gather.4.cloned.1.call-update) | async-done | bytes 4194320 | tf_op jit(solution)/shard_map/all_gather | solution.py:42
  45.1 7.2 %reshape.135 = bf16[1024,2048]{1,0:T(8,128)(2,1)} reshape(bf16[512,2,2048]{2,1,0:T(2,128)(2,1)} %all-gather.4.cloned.1.call-done) | data formatting | bytes 8388608 | tf_op jit(solution)/shard_map/reshape | solution.py:45
  52.3 7.8 %fusion.33 = bf16[1024,768]{0,1:T(8,128)(2,1)} fusion(bf16[1024,2048]{1,0:T(8,128)(2,1)} %reshape.135, bf16[2048,256]{1,0:T(8,128)(2,1)} %param.17, bf16[2048,256]{1,0:T(8,128)(2,1)} %param.16, bf16[2048,256]{1,0:T(8,128)(2,1)} %param.15), kind=kOutput, calls=%fused_computation.46 | convolution fusion | flops 3231449088 | bytes 8912896 | tf_op jit(solution)/shard_map/dot_general | solution.py:44
  62.7 4.5 reshape.136
  74.5 66.3 %all-gather.6.cloned.1.call-done = bf16[8192,2,256]{2,1,0:T(2,128)(2,1)} async-done(((bf16[512,2,256]{2,1,0:T(2,128)(2,1)}), bf16[8192,2,256]{2,1,0:T(2,128)(2,1)}) %all-gather.6.cloned.1.call-update) | async-done | bytes 8388624 | tf_op jit(solution)/shard_map/all_gather | solution.py:61
  140.8 21.6 %reshape.149 = bf16[16,512,2,2,128]{4,3,2,1,0:T(2,128)(2,1)} reshape(bf16[8192,2,256]{2,1,0:T(2,128)(2,1)} %all-gather.6.cloned.1.call-done) | data formatting | bytes 16777216 | tf_op jit(solution)/shard_map/reshape | solution.py:66
  162.5 50.9 %all-gather.8.cloned.1.call-done = bf16[8192,2,256]{2,1,0:T(2,128)(2,1)} async-done(((bf16[512,2,256]{2,1,0:T(2,128)(2,1)}), bf16[8192,2,256]{2,1,0:T(2,128)(2,1)}) %all-gather.8.cloned.1.call-update) | async-done | bytes 8388624 | tf_op jit(solution)/shard_map/all_gather | solution.py:62
  213.3 21.6 %reshape.150 = bf16[16,512,2,2,128]{4,3,2,1,0:T(2,128)(2,1)} reshape(bf16[8192,2,256]{2,1,0:T(2,128)(2,1)} %all-gather.8.cloned.1.call-done) | data formatting | bytes 16777216 | tf_op jit(solution)/shard_map/reshape | solution.py:67
  234.9 227.6 %while.15 = (s32[]{:T(128)}, f32[2,2,512]{2,1,0:T(2,128)S(1)}, f32[2,2,512]{2,1,0:T(2,128)S(1)}, f32[2,2,512,128]{3,2,1,0:T(8,128)}, s32[16]{0:T(128)S(1)}, /*in...) while((s32[]{:T(128)}, f32[2,2,512]{2,1,0:T(2,128)S(1)}, ...), condition=%wide.region_3.4_spmd.clone, body=%wide.region_0.3_spmd.clone.sunk | while | flops 549203456 | bytes 35266736 | solution.py:93
  259.0 4.1 fusion.75
  273.2 4.1 fusion.75
  287.5 4.1 fusion.75
  301.7 4.1 fusion.75
  316.0 4.1 fusion.75
  330.2 4.1 fusion.75
  344.5 4.1 fusion.75
  358.7 4.1 fusion.75
  373.0 4.1 fusion.75
  387.2 4.1 fusion.75
  401.5 4.1 fusion.75
  415.7 4.1 fusion.75
  430.0 4.1 fusion.75
  444.2 4.1 fusion.75
  458.5 4.1 fusion.75
  466.5 4.5 convolution_convert_fusion
  471.9 34.2 %reduce-scatter.2.cloned.1.call-done = bf16[64,2,2048]{2,0,1:T(8,128)(2,1)} async-done(((bf16[512,2,2048]{2,0,1:T(8,128)(2,1)}), bf16[64,2,2048]{2,0,1:T(8,128)(2,1)}) %reduce-scatter.2.cloned.1.call-update) | async-done | bytes 524304 | tf_op jit(solution)/shard_map/reduce_scatter | solution.py:107
  518.5 40.4 %all_to_all.10 = bf16[128,4,2048]{2,1,0:T(4,128)(2,1)} all-to-all(bf16[128,4,2048]{2,1,0:T(4,128)(2,1)S(1)} %bitcast.83), channel_id=1, replica_groups=mesh['expert'=16,'head'=8] {'expert','head'}, dimensions={0} | all-to-all | bytes 4194304 | tf_op jit(solution)/shard_map/all_to_all | solution.py:133
  562.9 5.3 fusion.36
  568.1 7.6 %convolution_convert_fusion.1 = bf16[512,2048]{1,0:T(8,128)(2,1)} fusion(bf16[1,704,2048]{2,1,0:T(8,128)(2,1)S(1)} %copy-done, bf16[512,2048]{1,0:T(8,128)(2,1)} %reshape.144, bf16[1,704,2048]{2,1,0:T(8,128)(2,1)} %param.21, f32[704,512]{1,0:T(8,128)} %fusion.36), kind=kOutput, calls=%fused_computation.34 | convolution fusion | flops 2956001280 | bytes 11403264 | tf_op jit(solution)/shard_map/dot_general | solution.py:17
  575.8 4.1 reshape.145
  579.9 5.7 all-to-all-start.1
  591.5 24.4 %all-to-all-done.1 = bf16[128,4,2048]{2,1,0:T(4,128)(2,1)} async-done(((bf16[128,4,2048]{2,1,0:T(4,128)(2,1)}), bf16[128,4,2048]{2,1,0:T(4,128)(2,1)}, u32[]{:S(2)}, u32[]{:S(2)}) %all-to-all-start.1) | async-done | bytes 2097184 | tf_op jit(solution)/shard_map/all_to_all | solution.py:137
  (229 shorter events, 212.7 us)
Async XLA Ops:
  6.5 561.6 %copy-start = (bf16[1,704,2048]{2,1,0:T(8,128)(2,1)S(1)}, bf16[1,704,2048]{2,1,0:T(8,128)(2,1)}, u32[]{:S(2)}) copy-start(bf16[1,704,2048]{2,1,0:T(8,128)(2,1)} %param.22) | copy-start | bytes 8650756
  6.5 38.5 %all-gather.4.cloned.1.call-start = ((), (), s32[]{:S(2)}) async-start(), calls=%async_computation.3 | async-start | bytes 4718592 | tf_op jit(solution)/shard_map/all_gather | solution.py:42
  7.3 133.5 %all-gather.6.cloned.1.call-start = ((), (), s32[]{:S(2)}) async-start(), calls=%async_computation.4 | async-start | bytes 8912896 | tf_op jit(solution)/shard_map/all_gather | solution.py:61
  62.7 9.0 %copy-start.3 = (s32[2]{0:T(128)S(1)}, s32[2]{0:T(128)}, u32[]{:S(2)}) copy-start(s32[2]{0:T(128)} %param.23) | copy-start | bytes 28
  70.7 142.7 %all-gather.8.cloned.1.call-start = ((), (), s32[]{:S(2)}) async-start(), calls=%async_computation.5 | async-start | bytes 8912896 | tf_op jit(solution)/shard_map/all_gather | solution.py:62
  71.4 434.7 %reduce-scatter.2.cloned.1.call-start = ((), (), s32[]{:S(2)}) async-start(), calls=%async_computation.6 | async-start | bytes 4718592 | tf_op jit(solution)/shard_map/reduce_scatter | solution.py:107
  241.6 3.4 copy-start.1
  255.5 3.4 copy-start.1
  269.8 3.4 copy-start.1
  284.0 3.4 copy-start.1
  298.3 3.4 copy-start.1
  312.5 3.4 copy-start.1
  326.8 3.4 copy-start.1
  341.0 3.4 copy-start.1
  355.3 3.4 copy-start.1
  369.5 3.4 copy-start.1
  383.8 3.4 copy-start.1
  398.0 3.4 copy-start.1
  412.3 3.4 copy-start.1
  426.5 3.4 copy-start.1
  440.8 3.4 copy-start.1
  455.0 3.4 copy-start.1
  471.0 0.7 copy-start.4
  471.0 0.7 copy-start.5
  471.0 0.7 copy-start.6
  471.0 35.2 %copy-start.2 = (bf16[64,2,2048]{2,1,0:T(2,128)(2,1)S(1)}, bf16[64,2,2048]{2,1,0:T(2,128)(2,1)}, u32[]{:S(2)}) copy-start(bf16[64,2,2048]{2,1,0:T(2,128)(2,1)} %param.14) | copy-start | bytes 1572868
  579.9 36.0 %all-to-all-start.1 = ((bf16[128,4,2048]{2,1,0:T(4,128)(2,1)}), bf16[128,4,2048]{2,1,0:T(4,128)(2,1)}, u32[]{:S(2)}, u32[]{:S(2)}) async-start(bf16[128,4,2048]{2,1,0:T(4,128)(2,1)} %reshape.145), calls=%async_computation.2 | async-start | bytes 4194304 | tf_op jit(solution)/shard_map/all_to_all | solution.py:137
Sparse Core Ops, SparseCore 0:
  9.1 35.9 all-gather.3
  70.8 69.9 all-gather.5
  143.0 70.3 all-gather.7
  471.1 34.9 reduce-scatter.1
where the time goes:
time: 635 us; the launch traced here: 632 us
  waiting for transfers between devices  215 us (34%)
  local copies, waits for them, and re-layouts  146 us (23%)
  matrix products  138 us (22%)
  other arithmetic  73.5 us (12%)
  blocking collectives  40.4 us (6%)
  between operations  13.2 us (2%)
    all_gather x1, waiting for transfers between devices, shards(): key_piece = lax.all_gather(key_rows, 'expert', axis=0, tiled=True)  66.3 us
    dot_general x16, matrix products, step(): jnp.einsum('shqk,kshd->shqd', exp_scores.astype(jnp.bfloat16), value_bloc...  65.2 us
    dynamic_slice x32, local copies, waits for them, and re-layouts, shards(): lax.scan(step, start_state, (key_blocks, value_blocks, block_starts))  52.7 us
    reduce_sum x16, other arithmetic, step(): running_sum = running_sum * factor + jnp.sum(exp_scores, axis=-1)  52.1 us
    all_gather x1, waiting for transfers between devices, shards(): value_piece = lax.all_gather(value_rows, 'expert', axis=0, tiled=True)  50.9 us
    dot_general x16, matrix products, step(): jnp.einsum('qshd,kshd->shqk', queries, key_block, preferred_element_type=...  42.8 us
    all_to_all x1, blocking collectives, shards(): lax.all_to_all(doubled, ('expert', 'head'), split_axis=0, concat_axis=0,...  40.4 us
    all_gather x1, waiting for transfers between devices, shards(): shard_rows = lax.all_gather(table_cells, 'head', axis=0, tiled=True)  37.8 us
  transfers between devices with their start and end apart: 5, of which 5 were waited for; matrix products, arithmetic and copies ran while one was open for 5% of the time, Pallas kernels for 0%

commit v1 on v0

--- a/solution.py
+++ b/solution.py
@@ -5,6 +5,16 @@
 from jax.sharding import PartitionSpec as P
 
 DH = 128
+
+
+def pass_along(shard, axis, dim):
+    n_dev = lax.axis_size(axis)
+    current, blocks = (shard, [shard])
+    for _ in range(n_dev - 1):
+        current = lax.ppermute(current, axis, [(i, (i + 1) % n_dev) for i in range(n_dev)])
+        blocks.insert(0, current)
+    flat = jnp.concatenate(blocks, axis=dim)
+    return jnp.roll(flat, (lax.axis_index(axis) + 1) * shard.shape[dim], axis=dim)
 
 
 def expert_half(slot_rows, gate_half, up_half, down_half):
@@ -58,7 +68,7 @@
         jnp.zeros((tables, head_count, row_cells), jnp.float32),
         jnp.zeros((tables, head_count, row_cells, DH), jnp.float32),
     )
-    key_piece = lax.all_gather(key_rows, "expert", axis=0, tiled=True)
+    key_piece = pass_along(key_rows, "expert", 0)
     value_piece = lax.all_gather(value_rows, "expert", axis=0, tiled=True)
     piece_len = key_piece.shape[0]
     block_len = math.gcd(piece_len, 512)

time: 635 us -> 838 us (1.32)
  waiting for transfers between devices: 215 us -> 359 us
  local copies, waits for them, and re-layouts: 146 us -> 179 us
  matrix products: 138 us -> 156 us
    ppermute x0 -> x15, waiting for transfers between devices: none -> 214 us  [pass_along(): lax.ppermute(current, axis, [(i, (i + 1) % n_dev) for i in range(n_dev)])]
    all_gather x1 -> x0, waiting for transfers between devices: 66.3 us -> none  [shards(): key_piece = lax.all_gather(key_rows, 'expert', axis=0, tiled=True)]
    unnamed x13 -> x48, local copies, waits for them, and re-layouts: 2 us -> 29.3 us
    dot_general x16, matrix products: 65.2 us -> 84.2 us  [step(): jnp.einsum('shqk,kshd->shqd', exp_scores.astype(jnp.bfloat16), value_bloc...]
  transfers between devices with their start and end apart: 5 -> 19, of which waited for: 5 -> 19; matrix products, arithmetic and copies ran while one was open for 5% -> 5% of each run, Pallas kernels for 0% -> 0%
where the time goes in v1:
time: 838 us; the launch traced here: 827 us
  waiting for transfers between devices  359 us (43%)
  local copies, waits for them, and re-layouts  179 us (21%)
  matrix products  156 us (19%)
  other arithmetic  71 us (8%)
  blocking collectives  40.4 us (5%)
  between operations  13.8 us (2%)
    ppermute x15, waiting for transfers between devices, pass_along(): lax.ppermute(current, axis, [(i, (i + 1) % n_dev) for i in range(n_dev)])  214 us
    dot_general x16, matrix products, step(): jnp.einsum('shqk,kshd->shqd', exp_scores.astype(jnp.bfloat16), value_bloc...  84.2 us
    dynamic_slice x32, local copies, waits for them, and re-layouts, shards(): lax.scan(step, start_state, (key_blocks, value_blocks, block_starts))  52.7 us
    reduce_sum x16, other arithmetic, step(): running_sum = running_sum * factor + jnp.sum(exp_scores, axis=-1)  49.7 us
    all_gather x1, waiting for transfers between devices, shards(): value_piece = lax.all_gather(value_rows, 'expert', axis=0, tiled=True)  47.3 us
    dot_general x16, matrix products, step(): jnp.einsum('qshd,kshd->shqk', queries, key_block, preferred_element_type=...  42.7 us
    all_to_all x1, blocking collectives, shards(): lax.all_to_all(doubled, ('expert', 'head'), split_axis=0, concat_axis=0,...  40.4 us
    all_gather x1, waiting for transfers between devices, shards(): shard_rows = lax.all_gather(table_cells, 'head', axis=0, tiled=True)  37.8 us
  transfers between devices with their start and end apart: 19, of which 19 were waited for; matrix products, arithmetic and copies ran while one was open for 5% of the time, Pallas kernels for 0%

profile of v1, /device:TPU:1, one launch (start us, length us, event | category | flops | bytes accessed | tf_op | source)
XLA Modules:
  0.0 827.1 jit_solution(1955717727188153227)
XLA Ops:
  7.3 37.8 %all-gather.3.cloned.1.call-done = bf16[512,2,2048]{2,1,0:T(2,128)(2,1)} async-done(((bf16[64,2,2048]{2,1,0:T(2,128)(2,1)}), bf16[512,2,2048]{2,1,0:T(2,128)(2,1)}) %all-gather.3.cloned.1.call-update) | async-done | bytes 4194320 | tf_op jit(solution)/shard_map/all_gather | solution.py:52
  45.1 7.2 reshape.135
  52.2 7.8 fusion.33
  70.0 15.4 %collective-permute-done = bf16[512,2,256]{2,1,0:T(2,128)(2,1)S(1)} collective-permute-done((bf16[512,2,256]{2,1,0:T(2,128)(2,1)S(1)}, bf16[512,2,256]{2,1,0:T(2,128)(2,1)S(1)}, u32[]{:S(2)}, u32[]{:S(2)}) %collective-permute-start) | collective-permute-done | bytes 524320 | tf_op jit(solution)/shard_map/ppermute | solution.py:14
  85.3 15.7 %collective-permute-done.1 = bf16[512,2,256]{2,1,0:T(2,128)(2,1)S(1)} collective-permute-done((bf16[512,2,256]{2,1,0:T(2,128)(2,1)S(1)}, bf16[512,2,256]{2,1,0:T(2,128)(2,1)S(1)}, u32[]{:S(2)}, u32[]{:S(2)}) %collective-permute-start.1) | collective-permute-done | bytes 524320 | tf_op jit(solution)/shard_map/ppermute | solution.py:14
  101.0 14.7 %collective-permute-done.2 = bf16[512,2,256]{2,1,0:T(2,128)(2,1)S(1)} collective-permute-done((bf16[512,2,256]{2,1,0:T(2,128)(2,1)S(1)}, bf16[512,2,256]{2,1,0:T(2,128)(2,1)S(1)}, u32[]{:S(2)}, u32[]{:S(2)}) %collective-permute-start.2) | collective-permute-done | bytes 524320 | tf_op jit(solution)/shard_map/ppermute | solution.py:14
  115.8 13.8 %collective-permute-done.3 = bf16[512,2,256]{2,1,0:T(2,128)(2,1)S(1)} collective-permute-done((bf16[512,2,256]{2,1,0:T(2,128)(2,1)S(1)}, bf16[512,2,256]{2,1,0:T(2,128)(2,1)S(1)}, u32[]{:S(2)}, u32[]{:S(2)}) %collective-permute-start.3) | collective-permute-done | bytes 524320 | tf_op jit(solution)/shard_map/ppermute | solution.py:14
  129.6 12.9 %collective-permute-done.4 = bf16[512,2,256]{2,1,0:T(2,128)(2,1)S(1)} collective-permute-done((bf16[512,2,256]{2,1,0:T(2,128)(2,1)S(1)}, bf16[512,2,256]{2,1,0:T(2,128)(2,1)S(1)}, u32[]{:S(2)}, u32[]{:S(2)}) %collective-permute-start.4) | collective-permute-done | bytes 524320 | tf_op jit(solution)/shard_map/ppermute | solution.py:14
  142.5 12.0 %collective-permute-done.5 = bf16[512,2,256]{2,1,0:T(2,128)(2,1)S(1)} collective-permute-done((bf16[512,2,256]{2,1,0:T(2,128)(2,1)S(1)}, bf16[512,2,256]{2,1,0:T(2,128)(2,1)S(1)}, u32[]{:S(2)}, u32[]{:S(2)}) %collective-permute-start.5) | collective-permute-done | bytes 524320 | tf_op jit(solution)/shard_map/ppermute | solution.py:14
  154.4 11.3 %collective-permute-done.6 = bf16[512,2,256]{2,1,0:T(2,128)(2,1)S(1)} collective-permute-done((bf16[512,2,256]{2,1,0:T(2,128)(2,1)S(1)}, bf16[512,2,256]{2,1,0:T(2,128)(2,1)S(1)}, u32[]{:S(2)}, u32[]{:S(2)}) %collective-permute-start.6) | collective-permute-done | bytes 524320 | tf_op jit(solution)/shard_map/ppermute | solution.py:14
  165.8 11.8 %collective-permute-done.7 = bf16[512,2,256]{2,1,0:T(2,128)(2,1)S(1)} collective-permute-done((bf16[512,2,256]{2,1,0:T(2,128)(2,1)S(1)}, bf16[512,2,256]{2,1,0:T(2,128)(2,1)S(1)}, u32[]{:S(2)}, u32[]{:S(2)}) %collective-permute-start.7) | collective-permute-done | bytes 524320 | tf_op jit(solution)/shard_map/ppermute | solution.py:14
  177.6 12.8 %collective-permute-done.8 = bf16[512,2,256]{2,1,0:T(2,128)(2,1)S(1)} collective-permute-done((bf16[512,2,256]{2,1,0:T(2,128)(2,1)S(1)}, bf16[512,2,256]{2,1,0:T(2,128)(2,1)S(1)}, u32[]{:S(2)}, u32[]{:S(2)}) %collective-permute-start.8) | collective-permute-done | bytes 524320 | tf_op jit(solution)/shard_map/ppermute | solution.py:14
  190.4 13.9 %collective-permute-done.9 = bf16[512,2,256]{2,1,0:T(2,128)(2,1)S(1)} collective-permute-done((bf16[512,2,256]{2,1,0:T(2,128)(2,1)S(1)}, bf16[512,2,256]{2,1,0:T(2,128)(2,1)S(1)}, u32[]{:S(2)}, u32[]{:S(2)}) %collective-permute-start.9) | collective-permute-done | bytes 524320 | tf_op jit(solution)/shard_map/ppermute | solution.py:14
  204.3 15.0 %collective-permute-done.10 = bf16[512,2,256]{2,1,0:T(2,128)(2,1)S(1)} collective-permute-done((bf16[512,2,256]{2,1,0:T(2,128)(2,1)S(1)}, bf16[512,2,256]{2,1,0:T(2,128)(2,1)S(1)}, u32[]{:S(2)}, u32[]{:S(2)}) %collective-permute-start.10) | collective-permute-done | bytes 524320 | tf_op jit(solution)/shard_map/ppermute | solution.py:14
  219.3 16.1 %collective-permute-done.11 = bf16[512,2,256]{2,1,0:T(2,128)(2,1)S(1)} collective-permute-done((bf16[512,2,256]{2,1,0:T(2,128)(2,1)S(1)}, bf16[512,2,256]{2,1,0:T(2,128)(2,1)S(1)}, u32[]{:S(2)}, u32[]{:S(2)}) %collective-permute-start.11) | collective-permute-done | bytes 524320 | tf_op jit(solution)/shard_map/ppermute | solution.py:14
  235.4 17.0 %collective-permute-done.12 = bf16[512,2,256]{2,1,0:T(2,128)(2,1)S(1)} collective-permute-done((bf16[512,2,256]{2,1,0:T(2,128)(2,1)S(1)}, bf16[512,2,256]{2,1,0:T(2,128)(2,1)S(1)}, u32[]{:S(2)}, u32[]{:S(2)}) %collective-permute-start.12) | collective-permute-done | bytes 524320 | tf_op jit(solution)/shard_map/ppermute | solution.py:14
  252.4 16.1 %collective-permute-done.13 = bf16[512,2,256]{2,1,0:T(2,128)(2,1)S(1)} collective-permute-done((bf16[512,2,256]{2,1,0:T(2,128)(2,1)S(1)}, bf16[512,2,256]{2,1,0:T(2,128)(2,1)S(1)}, u32[]{:S(2)}, u32[]{:S(2)}) %collective-permute-start.13) | collective-permute-done | bytes 524320 | tf_op jit(solution)/shard_map/ppermute | solution.py:14
  268.8 15.4 %collective-permute-done.14 = bf16[512,2,256]{2,1,0:T(2,128)(2,1)S(1)} collective-permute-done((bf16[512,2,256]{2,1,0:T(2,128)(2,1)S(1)}, bf16[512,2,256]{2,1,0:T(2,128)(2,1)S(1)}, u32[]{:S(2)}, u32[]{:S(2)}) %collective-permute-start.14) | collective-permute-done | bytes 524320 | tf_op jit(solution)/shard_map/ppermute | solution.py:14
  295.4 10.2 %constant_dynamic-update-slice_fusion.3 = bf16[16384,2,256]{2,1,0:T(2,128)(2,1)S(1)} fusion(bf16[16384,2,256]{2,1,0:T(2,128)(2,1)S(1)} %constant_dynamic-update-slice_fusion.4, bf16[512,2,256]{2,1,0:T(2,128)(2,1)S(1)} %collective-permute-done.2), kind=kLoop, calls=%fused_computation.61 | loop fusion | bytes 1048576
  308.4 5.7 copy-done.2
  314.3 8.0 constant_dynamic-slice_fusion.2
  322.3 21.7 %reshape.149 = bf16[16,512,2,2,128]{4,3,2,1,0:T(2,128)(2,1)} reshape(bf16[8192,2,256]{2,1,0:T(2,128)(2,1)} %constant_dynamic-slice_fusion.2) | data formatting | bytes 16777216 | tf_op jit(solution)/shard_map/reshape | solution.py:76
  346.8 47.3 %all-gather.5.cloned.1.call-done = bf16[8192,2,256]{2,1,0:T(2,128)(2,1)} async-done(((bf16[512,2,256]{2,1,0:T(2,128)(2,1)}), bf16[8192,2,256]{2,1,0:T(2,128)(2,1)}) %all-gather.5.cloned.1.call-update) | async-done | bytes 8388624 | tf_op jit(solution)/shard_map/all_gather | solution.py:72
  394.0 21.6 %reshape.150 = bf16[16,512,2,2,128]{4,3,2,1,0:T(2,128)(2,1)} reshape(bf16[8192,2,256]{2,1,0:T(2,128)(2,1)} %all-gather.5.cloned.1.call-done) | data formatting | bytes 16777216 | tf_op jit(solution)/shard_map/reshape | solution.py:77
  415.6 241.8 %while.15 = (s32[]{:T(128)}, f32[2,2,512]{2,1,0:T(2,128)S(1)}, f32[2,2,512]{2,1,0:T(2,128)S(1)}, f32[2,2,512,128]{3,2,1,0:T(8,128)}, s32[16]{0:T(128)S(1)}, /*in...) while((s32[]{:T(128)}, f32[2,2,512]{2,1,0:T(2,128)S(1)}, ...), condition=%wide.region_3.4_spmd.clone, body=%wide.region_0.3_spmd.clone.sunk | while | flops 549203456 | bytes 18489492 | solution.py:103
  440.3 5.3 fusion.75
  666.2 34.8 %reduce-scatter.2.cloned.1.call-done = bf16[64,2,2048]{2,0,1:T(8,128)(2,1)} async-done(((bf16[512,2,2048]{2,0,1:T(8,128)(2,1)}), bf16[64,2,2048]{2,0,1:T(8,128)(2,1)}) %reduce-scatter.2.cloned.1.call-update) | async-done | bytes 524304 | tf_op jit(solution)/shard_map/reduce_scatter | solution.py:117
  713.6 40.4 %all_to_all.10 = bf16[128,4,2048]{2,1,0:T(4,128)(2,1)} all-to-all(bf16[128,4,2048]{2,1,0:T(4,128)(2,1)S(1)} %bitcast.83), channel_id=1, replica_groups=mesh['expert'=16,'head'=8] {'expert','head'}, dimensions={0} | all-to-all | bytes 4194304 | tf_op jit(solution)/shard_map/all_to_all | solution.py:143
  757.9 5.3 fusion.36
  763.2 7.6 convolution_convert_fusion.1
  775.0 5.7 all-to-all-start.1
  786.6 24.3 %all-to-all-done.1 = bf16[128,4,2048]{2,1,0:T(4,128)(2,1)} async-done(((bf16[128,4,2048]{2,1,0:T(4,128)(2,1)}), bf16[128,4,2048]{2,1,0:T(4,128)(2,1)}, u32[]{:S(2)}, u32[]{:S(2)}) %all-to-all-start.1) | async-done | bytes 2097184 | tf_op jit(solution)/shard_map/all_to_all | solution.py:147
  (261 shorter events, 308.5 us)
Async XLA Ops:
  6.5 756.7 %copy-start = (bf16[1,704,2048]{2,1,0:T(8,128)(2,1)S(1)}, bf16[1,704,2048]{2,1,0:T(8,128)(2,1)}, u32[]{:S(2)}) copy-start(bf16[1,704,2048]{2,1,0:T(8,128)(2,1)} %param.22) | copy-start | bytes 8650756
  6.5 38.5 %all-gather.3.cloned.1.call-start = ((), (), s32[]{:S(2)}) async-start(), calls=%async_computation.3 | async-start | bytes 4718592 | tf_op jit(solution)/shard_map/all_gather | solution.py:52
  7.3 386.8 %all-gather.5.cloned.1.call-start = ((), (), s32[]{:S(2)}) async-start(), calls=%async_computation.4 | async-start | bytes 8912896 | tf_op jit(solution)/shard_map/all_gather | solution.py:72
  67.2 223.0 %copy-start.1 = (bf16[512,2,768]{2,1,0:T(2,128)(2,1)S(1)}, bf16[512,2,768]{2,1,0:T(2,128)(2,1)}, u32[]{:S(2)}) copy-start(bf16[512,2,768]{2,1,0:T(2,128)(2,1)} %reshape.136) | copy-start | bytes 4718596
  68.7 16.7 %collective-permute-start = (bf16[512,2,256]{2,1,0:T(2,128)(2,1)S(1)}, bf16[512,2,256]{2,1,0:T(2,128)(2,1)S(1)}, u32[]{:S(2)}, u32[]{:S(2)}) collective-permute-start(bf16[512,2,256]{2,1,0:T(2,128)(2,1)S(1)} %slice.20), channel_id=1, source_target_pairs={{0,8},{8,16},{16,24},{24,32},{32,40},{40,48},{48,56},{56,64},{64,7... | collective-permute-start | bytes 1572872 | tf_op jit(solution)/shard_map/ppermute | solution.py:14
  85.3 15.7 %collective-permute-start.1 = (bf16[512,2,256]{2,1,0:T(2,128)(2,1)S(1)}, bf16[512,2,256]{2,1,0:T(2,128)(2,1)S(1)}, u32[]{:S(2)}, u32[]{:S(2)}) collective-permute-start(bf16[512,2,256]{2,1,0:T(2,128)(2,1)S(1)} %collective-permute-done), channel_id=1, source_target_pairs={{0,8},{8,16},{16,24},{24,32},{32,40},{40,48},{48,56},{56,64},{64,7... | collective-permute-start | bytes 1572872 | tf_op jit(solution)/shard_map/ppermute | solution.py:14
  101.0 14.7 %collective-permute-start.2 = (bf16[512,2,256]{2,1,0:T(2,128)(2,1)S(1)}, bf16[512,2,256]{2,1,0:T(2,128)(2,1)S(1)}, u32[]{:S(2)}, u32[]{:S(2)}) collective-permute-start(bf16[512,2,256]{2,1,0:T(2,128)(2,1)S(1)} %collective-permute-done.1), channel_id=1, source_target_pairs={{0,8},{8,16},{16,24},{24,32},{32,40},{40,48},{48,56},{56,64},{64,7... | collective-permute-start | bytes 1572872 | tf_op jit(solution)/shard_map/ppermute | solution.py:14
  115.7 13.8 %collective-permute-start.3 = (bf16[512,2,256]{2,1,0:T(2,128)(2,1)S(1)}, bf16[512,2,256]{2,1,0:T(2,128)(2,1)S(1)}, u32[]{:S(2)}, u32[]{:S(2)}) collective-permute-start(bf16[512,2,256]{2,1,0:T(2,128)(2,1)S(1)} %collective-permute-done.2), channel_id=1, source_target_pairs={{0,8},{8,16},{16,24},{24,32},{32,40},{40,48},{48,56},{56,64},{64,7... | collective-permute-start | bytes 1572872 | tf_op jit(solution)/shard_map/ppermute | solution.py:14
  129.6 12.9 %collective-permute-start.4 = (bf16[512,2,256]{2,1,0:T(2,128)(2,1)S(1)}, bf16[512,2,256]{2,1,0:T(2,128)(2,1)S(1)}, u32[]{:S(2)}, u32[]{:S(2)}) collective-permute-start(bf16[512,2,256]{2,1,0:T(2,128)(2,1)S(1)} %collective-permute-done.3), channel_id=1, source_target_pairs={{0,8},{8,16},{16,24},{24,32},{32,40},{40,48},{48,56},{56,64},{64,7... | collective-permute-start | bytes 1572872 | tf_op jit(solution)/shard_map/ppermute | solution.py:14
  142.5 12.0 %collective-permute-start.5 = (bf16[512,2,256]{2,1,0:T(2,128)(2,1)S(1)}, bf16[512,2,256]{2,1,0:T(2,128)(2,1)S(1)}, u32[]{:S(2)}, u32[]{:S(2)}) collective-permute-start(bf16[512,2,256]{2,1,0:T(2,128)(2,1)S(1)} %collective-permute-done.4), channel_id=1, source_target_pairs={{0,8},{8,16},{16,24},{24,32},{32,40},{40,48},{48,56},{56,64},{64,7... | collective-permute-start | bytes 1572872 | tf_op jit(solution)/shard_map/ppermute | solution.py:14
  154.4 11.4 %collective-permute-start.6 = (bf16[512,2,256]{2,1,0:T(2,128)(2,1)S(1)}, bf16[512,2,256]{2,1,0:T(2,128)(2,1)S(1)}, u32[]{:S(2)}, u32[]{:S(2)}) collective-permute-start(bf16[512,2,256]{2,1,0:T(2,128)(2,1)S(1)} %collective-permute-done.5), channel_id=1, source_target_pairs={{0,8},{8,16},{16,24},{24,32},{32,40},{40,48},{48,56},{56,64},{64,7... | collective-permute-start | bytes 1572872 | tf_op jit(solution)/shard_map/ppermute | solution.py:14
  165.8 11.8 %collective-permute-start.7 = (bf16[512,2,256]{2,1,0:T(2,128)(2,1)S(1)}, bf16[512,2,256]{2,1,0:T(2,128)(2,1)S(1)}, u32[]{:S(2)}, u32[]{:S(2)}) collective-permute-start(bf16[512,2,256]{2,1,0:T(2,128)(2,1)S(1)} %collective-permute-done.6), channel_id=1, source_target_pairs={{0,8},{8,16},{16,24},{24,32},{32,40},{40,48},{48,56},{56,64},{64,7... | collective-permute-start | bytes 1572872 | tf_op jit(solution)/shard_map/ppermute | solution.py:14
  177.6 12.8 %collective-permute-start.8 = (bf16[512,2,256]{2,1,0:T(2,128)(2,1)S(1)}, bf16[512,2,256]{2,1,0:T(2,128)(2,1)S(1)}, u32[]{:S(2)}, u32[]{:S(2)}) collective-permute-start(bf16[512,2,256]{2,1,0:T(2,128)(2,1)S(1)} %collective-permute-done.7), channel_id=1, source_target_pairs={{0,8},{8,16},{16,24},{24,32},{32,40},{40,48},{48,56},{56,64},{64,7... | collective-permute-start | bytes 1572872 | tf_op jit(solution)/shard_map/ppermute | solution.py:14
  190.4 13.9 %collective-permute-start.9 = (bf16[512,2,256]{2,1,0:T(2,128)(2,1)S(1)}, bf16[512,2,256]{2,1,0:T(2,128)(2,1)S(1)}, u32[]{:S(2)}, u32[]{:S(2)}) collective-permute-start(bf16[512,2,256]{2,1,0:T(2,128)(2,1)S(1)} %collective-permute-done.8), channel_id=1, source_target_pairs={{0,8},{8,16},{16,24},{24,32},{32,40},{40,48},{48,56},{56,64},{64,7... | collective-permute-start | bytes 1572872 | tf_op jit(solution)/shard_map/ppermute | solution.py:14
  204.3 15.0 %collective-permute-start.10 = (bf16[512,2,256]{2,1,0:T(2,128)(2,1)S(1)}, bf16[512,2,256]{2,1,0:T(2,128)(2,1)S(1)}, u32[]{:S(2)}, u32[]{:S(2)}) collective-permute-start(bf16[512,2,256]{2,1,0:T(2,128)(2,1)S(1)} %collective-permute-done.9), channel_id=1, source_target_pairs={{0,8},{8,16},{16,24},{24,32},{32,40},{40,48},{48,56},{56,64},{64,7... | collective-permute-start | bytes 1572872 | tf_op jit(solution)/shard_map/ppermute | solution.py:14
  219.3 16.1 %collective-permute-start.11 = (bf16[512,2,256]{2,1,0:T(2,128)(2,1)S(1)}, bf16[512,2,256]{2,1,0:T(2,128)(2,1)S(1)}, u32[]{:S(2)}, u32[]{:S(2)}) collective-permute-start(bf16[512,2,256]{2,1,0:T(2,128)(2,1)S(1)} %collective-permute-done.10), channel_id=1, source_target_pairs={{0,8},{8,16},{16,24},{24,32},{32,40},{40,48},{48,56},{56,64},{64,7... | collective-permute-start | bytes 1572872 | tf_op jit(solution)/shard_map/ppermute | solution.py:14
  235.4 17.0 %collective-permute-start.12 = (bf16[512,2,256]{2,1,0:T(2,128)(2,1)S(1)}, bf16[512,2,256]{2,1,0:T(2,128)(2,1)S(1)}, u32[]{:S(2)}, u32[]{:S(2)}) collective-permute-start(bf16[512,2,256]{2,1,0:T(2,128)(2,1)S(1)} %collective-permute-done.11), channel_id=1, source_target_pairs={{0,8},{8,16},{16,24},{24,32},{32,40},{40,48},{48,56},{56,64},{64,7... | collective-permute-start | bytes 1572872 | tf_op jit(solution)/shard_map/ppermute | solution.py:14
  252.4 16.1 %collective-permute-start.13 = (bf16[512,2,256]{2,1,0:T(2,128)(2,1)S(1)}, bf16[512,2,256]{2,1,0:T(2,128)(2,1)S(1)}, u32[]{:S(2)}, u32[]{:S(2)}) collective-permute-start(bf16[512,2,256]{2,1,0:T(2,128)(2,1)S(1)} %collective-permute-done.12), channel_id=1, source_target_pairs={{0,8},{8,16},{16,24},{24,32},{32,40},{40,48},{48,56},{56,64},{64,7... | collective-permute-start | bytes 1572872 | tf_op jit(solution)/shard_map/ppermute | solution.py:14
  268.5 15.7 %collective-permute-start.14 = (bf16[512,2,256]{2,1,0:T(2,128)(2,1)S(1)}, bf16[512,2,256]{2,1,0:T(2,128)(2,1)S(1)}, u32[]{:S(2)}, u32[]{:S(2)}) collective-permute-start(bf16[512,2,256]{2,1,0:T(2,128)(2,1)S(1)} %collective-permute-done.13), channel_id=1, source_target_pairs={{0,8},{8,16},{16,24},{24,32},{32,40},{40,48},{48,56},{56,64},{64,7... | collective-permute-start | bytes 1572872 | tf_op jit(solution)/shard_map/ppermute | solution.py:14
  291.8 22.5 %copy-start.4 = (s32[2]{0:T(128)S(1)}, s32[2]{0:T(128)}, u32[]{:S(2)}) copy-start(s32[2]{0:T(128)} %param.23) | copy-start | bytes 28
  308.4 5.7 copy-start.2
  314.1 386.9 %reduce-scatter.2.cloned.1.call-start = ((), (), s32[]{:S(2)}) async-start(), calls=%async_computation.5 | async-start | bytes 4718592 | tf_op jit(solution)/shard_map/reduce_scatter | solution.py:117
  657.4 8.5 %copy-start.5 = (bf16[2048]{0:T(1024)(128)(2,1)S(1)}, bf16[2048]{0:T(1024)(128)(2,1)}, u32[]{:S(2)}) copy-start(bf16[2048]{0:T(1024)(128)(2,1)} %param.19) | copy-start | bytes 12292
  657.4 8.5 %copy-start.6 = (s32[64,2]{0,1:T(2,128)S(1)}, s32[64,2]{0,1:T(2,128)}, u32[]{:S(2)}) copy-start(s32[64,2]{0,1:T(2,128)} %param.25) | copy-start | bytes 1540
  657.4 8.5 %copy-start.7 = (s32[64,2]{0,1:T(2,128)S(1)}, s32[64,2]{0,1:T(2,128)}, u32[]{:S(2)}) copy-start(s32[64,2]{0,1:T(2,128)} %param.24) | copy-start | bytes 1540
  657.4 43.6 %copy-start.3 = (bf16[64,2,2048]{2,1,0:T(2,128)(2,1)S(1)}, bf16[64,2,2048]{2,1,0:T(2,128)(2,1)}, u32[]{:S(2)}) copy-start(bf16[64,2,2048]{2,1,0:T(2,128)(2,1)} %param.14) | copy-start | bytes 1572868
  775.0 36.0 %all-to-all-start.1 = ((bf16[128,4,2048]{2,1,0:T(4,128)(2,1)}), bf16[128,4,2048]{2,1,0:T(4,128)(2,1)}, u32[]{:S(2)}, u32[]{:S(2)}) async-start(bf16[128,4,2048]{2,1,0:T(4,128)(2,1)} %reshape.145), calls=%async_computation.2 | async-start | bytes 4194304 | tf_op jit(solution)/shard_map/all_to_all | solution.py:147
Sparse Core Ops, SparseCore 0:
  9.1 35.9 all-gather.2
  314.2 79.7 all-gather.4
  666.1 34.9 reduce-scatter.1
